TPU v7x, 32 devices: a whole 2x2x4 slice. The times are simulated.
32 devices in a mesh: grp: 2 (over x), cand: 16 (over z, y, core).
Axes of the slice: x: 2, y: 2, z: 4, core: 2. Of those that a mesh axis runs over, the one named last changes fastest.
Arguments:
- prompt_key_rows: bfloat16 [256, 512], P(('grp', 'cand')), parts along dimension 0, may hold values from -6 to 6
- prompt_value_rows: bfloat16 [256, 512], P(('grp', 'cand')), parts along dimension 0, may hold values from -6 to 6
- queries: bfloat16 [4096, 4096], P(('grp', 'cand')), parts along dimension 0, may hold values from -6 to 6
- keys: bfloat16 [4096, 512], P(('grp', 'cand')), parts along dimension 0, may hold values from -6 to 6
- values: bfloat16 [4096, 512], P(('grp', 'cand')), parts along dimension 0, may hold values from -6 to 6
- output_gradient: bfloat16 [4096, 4096], P(('grp', 'cand')), parts along dimension 0, may hold values from -12 to 12
- lengths: int32 [32], P(('grp', 'cand')), parts along dimension 0, may hold values from 1 to 120, 640 in all
- prompt_visible_rows: int32 [32], P(('grp', 'cand')), parts along dimension 0, may hold values from 32 to 128
- query_gain: float32 [128], replicated, may hold values from 0.25 to 1.75
- key_norm_gain: float32 [128], replicated, may hold values from 0.25 to 1.75
- key_value_weight: bfloat16 [5120, 1024], P('cand'), may hold values from -0.25 to 0.25
Outputs:
- query_grad: bfloat16 [4096, 4096], P(('grp', 'cand')), parts along dimension 0
- key_grad: bfloat16 [4096, 512], P(('grp', 'cand')), parts along dimension 0
- value_grad: bfloat16 [4096, 512], P(('grp', 'cand')), parts along dimension 0
- prompt_hidden_grad: bfloat16 [256, 5120], P(('grp', 'cand')), parts along dimension 0
There are 2 independent parts, one for each index of `grp`. A program takes and returns all parts, laid end to end along the dimension named above; an argument that names none is the same for every part. Nothing has to cross between parts.
Inputs may be any that keep to these rules, and one draw needn't show every extreme that they name: The first lengths[c] of candidate c's 128 slots hold its response, the rest are padding.
All inputs are finite; a program needn't handle non-finite values. No bound on the sum of `lengths` on one device may be relied on, other than what follows from the above.
Results may differ from a plain program's by a relative error of at most 0.0098.
Values may be sent and summed in bfloat16 or wider, within the bound.
A program may use at most 128 MiB of HBM per device.

v0:
```python
import jax
import jax.numpy as jnp
from jax import lax
from jax.sharding import PartitionSpec as P

epsilon = 1e-06


def head_norm_forward(raw, gain, heads):
    count = raw.shape[0]
    inputs = raw.astype(jnp.float32).reshape(count, heads, -1)
    factor = lax.rsqrt(jnp.mean(inputs * inputs, axis=-1, keepdims=True) + epsilon)
    normed = (inputs * factor * gain).reshape(count, -1).astype(jnp.bfloat16)
    return (inputs, factor, normed)


def norm_backward(inputs, factor, gain, upstream):
    count = inputs.shape[0]
    scaled = upstream.reshape(inputs.shape) * gain
    inner = jnp.mean(scaled * inputs, axis=-1, keepdims=True)
    return (factor * scaled - inputs * (factor * factor * factor) * inner).reshape(count, -1)


def contract_rows(left, right):
    return lax.dot_general(
        left, right, (((0,), (0,)), ((), ())), preferred_element_type=jnp.float32
    )


def contract_last(left, right):
    return lax.dot_general(
        left, right, (((1,), (1,)), ((), ())), preferred_element_type=jnp.float32
    )


def attend(normed_q, all_keys, all_values, masked_grad, visible, head_dim):
    count = normed_q.shape[0]
    total = all_keys.shape[0]
    kv_heads = all_keys.shape[1] // head_dim
    group = normed_q.shape[1] // (kv_heads * head_dim)
    scale = head_dim ** (-0.5)
    weight_mask = visible.astype(jnp.float32)[:, None, :]
    q_parts, k_parts, v_parts = ([], [], [])
    for head in range(kv_heads):
        width = group * head_dim
        q_block = normed_q[:, head * width : (head + 1) * width].reshape(count * group, head_dim)
        g_block = masked_grad[:, head * width : (head + 1) * width].reshape(count * group, head_dim)
        k_block = all_keys[:, head * head_dim : (head + 1) * head_dim]
        v_block = all_values[:, head * head_dim : (head + 1) * head_dim]
        scores = contract_last(q_block, k_block).reshape(count, group, total) * scale
        expo = jnp.exp(scores) * weight_mask
        probs = expo / jnp.sum(expo, axis=-1, keepdims=True)
        probs_low = probs.astype(jnp.bfloat16).reshape(count * group, total)
        v_parts.append(contract_rows(probs_low, g_block))
        dprobs = contract_last(g_block, v_block).reshape(count, group, total)
        delta = jnp.sum(probs * dprobs, axis=-1, keepdims=True)
        dscore = (
            (probs * (dprobs - delta) * scale).astype(jnp.bfloat16).reshape(count * group, total)
        )
        q_parts.append(
            jnp.dot(dscore, k_block, preferred_element_type=jnp.float32).reshape(count, width)
        )
        k_parts.append(contract_rows(dscore, q_block))
    return (
        jnp.concatenate(q_parts, axis=1),
        jnp.concatenate(k_parts, axis=1),
        jnp.concatenate(v_parts, axis=1),
    )


def on_device(
    prompt_key_rows,
    prompt_value_rows,
    queries,
    keys,
    values,
    output_gradient,
    lengths,
    prompt_visible_rows,
    query_gain,
    key_norm_gain,
    key_value_weight,
):
    head_dim = query_gain.shape[0]
    kv_heads = keys.shape[1] // head_dim
    q_heads = queries.shape[1] // head_dim
    slots = queries.shape[0]
    gathered_keys, all_prompt_values = (
        lax.all_gather(prompt_key_rows, "cand", axis=0, tiled=True),
        lax.all_gather(prompt_value_rows, "cand", axis=0, tiled=True),
    )
    full_inputs, full_factor, all_prompt_keys = head_norm_forward(
        gathered_keys, key_norm_gain, kv_heads
    )
    prompt_total = all_prompt_keys.shape[0]
    q_inputs, q_factor, q_normed = head_norm_forward(queries, query_gain, q_heads)
    key_norm_inputs, key_norm_factor, key_after_norm = head_norm_forward(
        keys, key_norm_gain, kv_heads
    )
    slot_index = jnp.arange(slots, dtype=jnp.int32)
    prompt_index = jnp.arange(prompt_total, dtype=jnp.int32)
    masked_grad = jnp.where(
        (slot_index < lengths[0])[:, None], output_gradient, jnp.zeros_like(output_gradient)
    )
    prompt_visible = jnp.broadcast_to(
        (prompt_index < prompt_visible_rows[0])[None, :], (slots, prompt_total)
    )
    causal = slot_index[None, :] <= slot_index[:, None]
    visible = jnp.concatenate([prompt_visible, causal], axis=1)
    all_keys = jnp.concatenate([all_prompt_keys, key_after_norm], axis=0)
    all_values = jnp.concatenate([all_prompt_values, values], axis=0)
    dq_n, dk_n, dv_n = attend(q_normed, all_keys, all_values, masked_grad, visible, head_dim)
    query_grad = norm_backward(q_inputs, q_factor, query_gain, dq_n).astype(jnp.bfloat16)
    key_grad = norm_backward(
        key_norm_inputs, key_norm_factor, key_norm_gain, dk_n[prompt_total:]
    ).astype(jnp.bfloat16)
    value_grad = dv_n[prompt_total:].astype(jnp.bfloat16)
    total_dk, total_dv = lax.psum((dk_n[:prompt_total], dv_n[:prompt_total]), "cand")
    full_dk = norm_backward(full_inputs, full_factor, key_norm_gain, total_dk).astype(jnp.bfloat16)
    full_grads = jnp.concatenate([full_dk, total_dv.astype(jnp.bfloat16)], axis=1)
    slices = contract_last(key_value_weight, full_grads).astype(jnp.bfloat16)
    hidden_state = lax.all_to_all(slices, "cand", split_axis=1, concat_axis=0, tiled=True).T
    return (query_grad, key_grad, value_grad, hidden_state)


def solution(mesh):
    return jax.shard_map(
        on_device,
        mesh=mesh,
        in_specs=(
            P(("grp", "cand"), None),
            P(("grp", "cand"), None),
            P(("grp", "cand"), None),
            P(("grp", "cand"), None),
            P(("grp", "cand"), None),
            P(("grp", "cand"), None),
            P(("grp", "cand")),
            P(("grp", "cand")),
            P(),
            P(),
            P("cand", None),
        ),
        out_specs=(
            P(("grp", "cand"), None),
            P(("grp", "cand"), None),
            P(("grp", "cand"), None),
            P(("grp", "cand"), None),
        ),
        check_vma=False,
    )
```

profile of v0, /device:TPU:0, one launch (start us, length us, event | category | flops | bytes accessed | tf_op | source)
XLA Modules:
  0.0 215.4 jit_solution(11398596797263702017)
XLA Ops:
  8.7 1.2 broadcast_bitcast_fusion.1
  10.6 23.7 %all_gather.6 = bf16[128,512]{1,0:T(8,128)(2,1)S(1)} all-gather(bf16[8,512]{1,0:T(8,128)(2,1)} %param.11), channel_id=1, replica_groups=mesh['grp'=2,'cand'=16] {'cand'}, dimensions={0}, use_global_device_ids=true | all-gather | bytes 139264 | tf_op jit(solution)/shard_map/all_gather | solution.py:89
  34.3 18.0 %all_gather.7 = bf16[128,512]{1,0:T(8,128)(2,1)S(1)} all-gather(bf16[8,512]{1,0:T(8,128)(2,1)} %param.12), channel_id=1, replica_groups=mesh['grp'=2,'cand'=16] {'cand'}, dimensions={0}, use_global_device_ids=true | all-gather | bytes 139264 | tf_op jit(solution)/shard_map/all_gather | solution.py:90
  62.4 1.8 copy.156
  66.2 2.6 %fusion.130 = (bf16[128,8,256]{2,0,1:T(8,128)(2,1)}, f32[128,8,256]{2,0,1:T(8,128)}) fusion(bf16[128,8,128]{0,2,1:T(8,128)(2,1)} %bitcast.221, f32[128,256]{1,0:T(8,128)} %add_convert_fusion, bf16[128,512]{1,0:T(8,128)(2,1)S(1)} %get-tuple-element.42, bf16[128,512]{1,0:T(8,128)(2,1)S(1)} %get-tuple-element.43), kind=kOutput, calls=%fused_computation.173 | convolution fusion | flops 68289792 | bytes 2228224 | tf_op jit(solution)/shard_map/div | solution.py:52
  68.8 2.7 %fusion.127 = (bf16[128,8,256]{2,0,1:T(8,128)(2,1)}, f32[128,8,256]{2,0,1:T(8,128)}) fusion(bf16[128,8,128]{0,2,1:T(8,128)(2,1)} %bitcast.220, f32[128,256]{1,0:T(8,128)} %add_convert_fusion, bf16[128,512]{1,0:T(8,128)(2,1)S(1)} %get-tuple-element.42, bf16[128,512]{1,0:T(8,128)(2,1)S(1)} %get-tuple-element.43), kind=kOutput, calls=%fused_computation.172 | convolution fusion | flops 68289792 | bytes 2228224 | tf_op jit(solution)/shard_map/div | solution.py:52
  71.5 2.6 %fusion.133 = (bf16[128,8,256]{2,0,1:T(8,128)(2,1)}, f32[128,8,256]{2,0,1:T(8,128)}) fusion(bf16[128,8,128]{0,2,1:T(8,128)(2,1)S(1)} %bitcast.219, f32[128,256]{1,0:T(8,128)} %add_convert_fusion, bf16[128,512]{1,0:T(8,128)(2,1)S(1)} %get-tuple-element.42, bf16[128,512]{1,0:T(8,128)(2,1)S(1)} %get-tuple-element.43), kind=kOutput, calls=%fused_computation.174 | convolution fusion | flops 68289792 | bytes 2228224 | tf_op jit(solution)/shard_map/div | solution.py:52
  75.7 2.1 fusion.30
  77.8 2.3 %fusion.49 = f32[256,128]{1,0:T(8,128)} fusion(bf16[1024,128]{1,0:T(8,128)(2,1)} %reshape.240, bf16[128,8,256]{2,0,1:T(8,128)(2,1)S(1)} %fusion.30), kind=kOutput, calls=%fused_computation.69 | convolution fusion | flops 67108864 | bytes 917504 | tf_op jit(solution)/shard_map/dot_general | solution.py:25
  80.1 3.1 %fusion.29 = bf16[128,8,256]{2,0,1:T(8,128)(2,1)} fusion(f32[128,8,256]{2,0,1:T(8,128)} %get-tuple-element.47, bf16[128,8,128]{0,2,1:T(8,128)(2,1)S(1)} %bitcast.207, bf16[256,512]{1,0:T(8,128)(2,1)} %copy-done.19), kind=kOutput, calls=%fused_computation.41 | convolution fusion | flops 135529728 | bytes 3276800 | tf_op jit(solution)/shard_map/sub | solution.py:58
  83.2 2.3 %fusion.47 = f32[256,128]{1,0:T(8,128)} fusion(bf16[1024,128]{1,0:T(8,128)(2,1)} %reshape.242, bf16[128,8,256]{2,0,1:T(8,128)(2,1)} %fusion.29), kind=kOutput, calls=%fused_computation.67 | convolution fusion | flops 67108864 | bytes 917504 | tf_op jit(solution)/shard_map/dot_general | solution.py:25
  85.5 2.7 %fusion.126 = (bf16[128,8,256]{2,0,1:T(8,128)(2,1)}, f32[128,8,256]{2,0,1:T(8,128)}) fusion(bf16[128,8,128]{0,2,1:T(8,128)(2,1)} %bitcast.218, bf16[256,128,1]{1,0,2:T(8,128)(2,1)} %fusion.94, f32[128,256]{1,0:T(8,128)} %add_convert_fusion), kind=kOutput, calls=%fused_computation.171 | convolution fusion | flops 68158720 | bytes 2031616 | tf_op jit(solution)/shard_map/div | solution.py:52
  88.1 2.3 %fusion.28 = bf16[128,8,256]{2,0,1:T(8,128)(2,1)S(1)} fusion(f32[128,8,256]{2,0,1:T(8,128)} %get-tuple-element.45, bf16[128,8,128]{0,2,1:T(8,128)(2,1)S(1)} %bitcast.208, bf16[256,512]{1,0:T(8,128)(2,1)} %copy-done.19), kind=kOutput, calls=%fused_computation.40 | convolution fusion | flops 135529728 | bytes 3276800 | tf_op jit(solution)/shard_map/sub | solution.py:58
  90.4 2.3 %fusion.45 = f32[256,128]{1,0:T(8,128)} fusion(bf16[1024,128]{1,0:T(8,128)(2,1)} %reshape.244, bf16[128,8,256]{2,0,1:T(8,128)(2,1)S(1)} %fusion.28), kind=kOutput, calls=%fused_computation.65 | convolution fusion | flops 67108864 | bytes 917504 | tf_op jit(solution)/shard_map/dot_general | solution.py:25
  92.7 2.9 %fusion.31 = bf16[128,8,256]{2,0,1:T(8,128)(2,1)} fusion(f32[128,8,256]{2,0,1:T(8,128)} %get-tuple-element.51, bf16[128,8,128]{0,2,1:T(8,128)(2,1)S(1)} %bitcast.209, bf16[256,512]{1,0:T(8,128)(2,1)} %copy-done.19), kind=kOutput, calls=%fused_computation.43 | convolution fusion | flops 135529728 | bytes 3276800 | tf_op jit(solution)/shard_map/sub | solution.py:58
  95.6 1.6 fusion.51
  102.5 2.2 %fusion.110 = f32[128,8,128]{0,2,1:T(8,128)} fusion(bf16[128,8,256]{2,0,1:T(8,128)(2,1)} %copy-done.9, bf16[128,512]{1,0:T(8,128)(2,1)S(1)} %get-tuple-element.42, bf16[128,512]{1,0:T(8,128)(2,1)S(1)} %get-tuple-element.43), kind=kOutput, calls=%fused_computation.165 | convolution fusion | flops 67239936 | bytes 1310720 | tf_op jit(solution)/shard_map/dot_general | solution.py:61
  105.9 1.1 fusion.136
  107.0 1.1 fusion.115
  110.3 1.6 fusion.41
  111.9 1.5 fusion.39
  113.5 1.6 fusion.37
  117.0 1.4 copy.195
  118.4 1.4 copy.180
  120.6 3.9 %multiply_reduce_fusion = (f32[128,32]{0,1:T(8,128)}, f32[128,32,128]{0,2,1:T(8,128)}) fusion(f32[128]{0:T(128)} %param.19, bf16[128,4096]{0,1:T(8,128)(2,1)S(1)} %copy.150, f32[128,8,128]{0,2,1:T(8,128)} %fusion.136, f32[128,8,128]{0,2,1:T(8,128)} %fusion.120, f32[128,8,128]{0,2,1:T(8,128)S(1)} %copy-done.17, f32[128,8,128]{0,2,1:T(8,128)} %fusion.115), kind=kLoop, calls=%fused_computation.14 | loop fusion | flops 3665920 | bytes 5259776 | tf_op jit(solution)/shard_map/reduce_sum | solution.py:20
  124.5 63.0 %all-reduce.4 = bf16[128,512]{1,0:T(8,128)(2,1)} all-reduce(f32[128,512]{1,0:T(8,128)} %slice.102), channel_id=1, replica_groups=mesh['grp'=2,'cand'=16] {'cand'}, use_global_device_ids=true, to_apply=%region_15.16 | all-reduce | flops 65536 | bytes 393216 | tf_op jit(solution)/shard_map/psum | solution.py:118
  187.5 1.7 reshape.254
  189.2 1.4 multiply_reduce_fusion.6
  195.3 5.1 %all-to-all-start = ((bf16[320,16,8]{0,2,1:T(8,128)(2,1)}), bf16[320,16,8]{0,2,1:T(8,128)(2,1)S(1)}, u32[]{:S(2)}, u32[]{:S(2)}) async-start(bf16[320,16,8]{0,2,1:T(8,128)(2,1)} %bitcast.38), calls=%async_computation | async-start | bytes 196608 | tf_op jit(solution)/shard_map/all_to_all | solution.py:122
  201.1 2.0 fusion.7
  203.1 1.3 copy.200
  204.4 3.4 %all-to-all-done = bf16[320,16,8]{0,2,1:T(8,128)(2,1)S(1)} async-done(((bf16[320,16,8]{0,2,1:T(8,128)(2,1)}), bf16[320,16,8]{0,2,1:T(8,128)(2,1)S(1)}, u32[]{:S(2)}, u32[]{:S(2)}) %all-to-all-start) | async-done | bytes 81952 | tf_op jit(solution)/shard_map/all_to_all | solution.py:122
  (147 shorter events, 31.6 us)
Async XLA Ops:
  7.2 187.1 %copy-start = (bf16[320,1024]{1,0:T(8,128)(2,1)S(1)}, bf16[320,1024]{1,0:T(8,128)(2,1)}, u32[]{:S(2)}) copy-start(bf16[320,1024]{1,0:T(8,128)(2,1)} %param.21) | copy-start | bytes 1966084
  7.2 48.9 %copy-start.23 = (bf16[128,4096]{1,0:T(8,128)(2,1)S(1)}, bf16[128,4096]{1,0:T(8,128)(2,1)}, u32[]{:S(2)}) copy-start(bf16[128,4096]{1,0:T(8,128)(2,1)} %param.13) | copy-start | bytes 3145732
  7.2 180.3 %all-reduce.3.cloned.1.call-start = ((), (), s32[]{:S(2)}) async-start(), calls=%async_computation.1 | async-start | bytes 524288 | tf_op jit(solution)/shard_map/psum | solution.py:118
  10.6 47.0 %copy-start.35 = (f32[4096]{0:T(1024)}, f32[4096]{0:T(1024)S(1)}, u32[]{:S(2)}) copy-start(f32[4096]{0:T(1024)S(1)} %broadcast_bitcast_fusion) | copy-start | bytes 49156
  34.3 19.7 %copy-start.14 = (bf16[128,512]{1,0:T(8,128)(2,1)}, bf16[128,512]{1,0:T(8,128)(2,1)S(1)}, u32[]{:S(2)}) copy-start(bf16[128,512]{1,0:T(8,128)(2,1)S(1)} %all_gather.6) | copy-start | bytes 393220
  58.4 3.1 %copy-start.28 = (bf16[128,1024]{0,1:T(8,128)(2,1)}, bf16[128,1024]{0,1:T(8,128)(2,1)S(1)}, u32[]{:S(2)}) copy-start(bf16[128,1024]{0,1:T(8,128)(2,1)S(1)} %get-tuple-element.29) | copy-start | bytes 786436
  58.4 3.1 %copy-start.29 = (bf16[128,1024]{0,1:T(8,128)(2,1)}, bf16[128,1024]{0,1:T(8,128)(2,1)S(1)}, u32[]{:S(2)}) copy-start(bf16[128,1024]{0,1:T(8,128)(2,1)S(1)} %get-tuple-element.28) | copy-start | bytes 786436
  58.4 3.1 %copy-start.31 = (bf16[128,1024]{0,1:T(8,128)(2,1)}, bf16[128,1024]{0,1:T(8,128)(2,1)S(1)}, u32[]{:S(2)}) copy-start(bf16[128,1024]{0,1:T(8,128)(2,1)S(1)} %get-tuple-element.30) | copy-start | bytes 786436
  58.4 3.9 %copy-start.32 = (bf16[128,1024]{0,1:T(8,128)(2,1)}, bf16[128,1024]{0,1:T(8,128)(2,1)S(1)}, u32[]{:S(2)}) copy-start(bf16[128,1024]{0,1:T(8,128)(2,1)S(1)} %get-tuple-element.31) | copy-start | bytes 786436
  65.2 3.6 %copy-start.1 = (f32[128,4,128]{2,1,0:T(4,128)}, f32[128,4,128]{2,1,0:T(4,128)S(1)}, u32[]{:S(2)}) copy-start(f32[128,4,128]{2,1,0:T(4,128)S(1)} %mul.333) | copy-start | bytes 786436
  65.4 3.4 %copy-start.3 = (f32[128,4,128]{2,1,0:T(4,128)}, f32[128,4,128]{2,1,0:T(4,128)S(1)}, u32[]{:S(2)}) copy-start(f32[128,4,128]{2,1,0:T(4,128)S(1)} %mul.341) | copy-start | bytes 786436
  77.8 10.3 %copy-start.9 = (bf16[128,8,256]{2,0,1:T(8,128)(2,1)}, bf16[128,8,256]{2,0,1:T(8,128)(2,1)S(1)}, u32[]{:S(2)}) copy-start(bf16[128,8,256]{2,0,1:T(8,128)(2,1)S(1)} %fusion.30) | copy-start | bytes 1572868
  90.4 5.2 %copy-start.11 = (bf16[128,8,256]{2,0,1:T(8,128)(2,1)}, bf16[128,8,256]{2,0,1:T(8,128)(2,1)S(1)}, u32[]{:S(2)}) copy-start(bf16[128,8,256]{2,0,1:T(8,128)(2,1)S(1)} %fusion.28) | copy-start | bytes 1572868
  100.8 4.0 %copy-start.10 = (bf16[128,8,256]{2,0,1:T(8,128)(2,1)S(1)}, bf16[128,8,256]{2,0,1:T(8,128)(2,1)}, u32[]{:S(2)}) copy-start(bf16[128,8,256]{2,0,1:T(8,128)(2,1)} %fusion.29) | copy-start | bytes 1572868
  102.5 3.4 %copy-start.12 = (bf16[128,8,256]{2,0,1:T(8,128)(2,1)S(1)}, bf16[128,8,256]{2,0,1:T(8,128)(2,1)}, u32[]{:S(2)}) copy-start(bf16[128,8,256]{2,0,1:T(8,128)(2,1)} %copy-done.11) | copy-start | bytes 1572868
  102.5 3.4 %copy-start.33 = (bf16[256,128,1]{1,0,2:T(8,128)(2,1)S(1)}, bf16[256,128,1]{1,0,2:T(8,128)(2,1)}, u32[]{:S(2)}) copy-start(bf16[256,128,1]{1,0,2:T(8,128)(2,1)} %fusion.94) | copy-start | bytes 196612
  102.5 4.5 %copy-start.13 = (bf16[128,8,256]{2,0,1:T(8,128)(2,1)S(1)}, bf16[128,8,256]{2,0,1:T(8,128)(2,1)}, u32[]{:S(2)}) copy-start(bf16[128,8,256]{2,0,1:T(8,128)(2,1)} %fusion.31) | copy-start | bytes 1572868
  107.0 3.2 %copy-start.26 = (bf16[128,1024]{1,0:T(8,128)(2,1)S(1)}, bf16[128,1024]{1,0:T(8,128)(2,1)}, u32[]{:S(2)}) copy-start(bf16[128,1024]{1,0:T(8,128)(2,1)} %copy.186) | copy-start | bytes 786436
  109.1 4.4 %copy-start.34 = (bf16[1024,128]{1,0:T(8,128)(2,1)S(1)}, bf16[1024,128]{1,0:T(8,128)(2,1)}, u32[]{:S(2)}) copy-start(bf16[1024,128]{1,0:T(8,128)(2,1)} %reshape.253) | copy-start | bytes 786436
  110.3 4.8 %copy-start.39 = (bf16[128,8,256]{2,0,1:T(8,128)(2,1)S(1)}, bf16[128,8,256]{2,0,1:T(8,128)(2,1)}, u32[]{:S(2)}) copy-start(bf16[128,8,256]{2,0,1:T(8,128)(2,1)} %get-tuple-element.50) | copy-start | bytes 1572868
  113.5 6.4 %copy-start.27 = (f32[128,512]{1,0:T(8,128)S(1)}, f32[128,512]{1,0:T(8,128)}, u32[]{:S(2)}) copy-start(f32[128,512]{1,0:T(8,128)} %get-tuple-element.32) | copy-start | bytes 786436
  113.5 7.2 %copy-start.17 = (f32[128,8,128]{0,2,1:T(8,128)S(1)}, f32[128,8,128]{0,2,1:T(8,128)}, u32[]{:S(2)}) copy-start(f32[128,8,128]{0,2,1:T(8,128)} %fusion.110) | copy-start | bytes 1572868
  120.6 68.6 %copy-start.6 = (f32[128,4,128]{2,1,0:T(4,128)S(1)}, f32[128,4,128]{2,1,0:T(4,128)}, u32[]{:S(2)}) copy-start(f32[128,4,128]{2,1,0:T(4,128)} %copy-done.5) | copy-start | bytes 786436
  120.6 68.6 %copy-start.8 = (f32[128,4,128]{2,1,0:T(4,128)S(1)}, f32[128,4,128]{2,1,0:T(4,128)}, u32[]{:S(2)}) copy-start(f32[128,4,128]{2,1,0:T(4,128)} %copy-done.7) | copy-start | bytes 786436
  124.5 68.7 %copy-start.2 = (f32[128,4,128]{2,1,0:T(4,128)S(1)}, f32[128,4,128]{2,1,0:T(4,128)}, u32[]{:S(2)}) copy-start(f32[128,4,128]{2,1,0:T(4,128)} %copy-done.1) | copy-start | bytes 786436
  124.5 68.7 %copy-start.4 = (f32[128,4,128]{2,1,0:T(4,128)S(1)}, f32[128,4,128]{2,1,0:T(4,128)}, u32[]{:S(2)}) copy-start(f32[128,4,128]{2,1,0:T(4,128)} %copy-done.3) | copy-start | bytes 786436
  124.5 68.7 %copy-start.16 = (bf16[128,512]{1,0:T(8,128)(2,1)S(1)}, bf16[128,512]{1,0:T(8,128)(2,1)}, u32[]{:S(2)}) copy-start(bf16[128,512]{1,0:T(8,128)(2,1)} %copy-done.14) | copy-start | bytes 393220
  124.5 68.7 %copy-start.21 = (bf16[128,512]{1,0:T(8,128)(2,1)S(1)}, bf16[128,512]{1,0:T(8,128)(2,1)}, u32[]{:S(2)}) copy-start(bf16[128,512]{1,0:T(8,128)(2,1)} %param.14) | copy-start | bytes 393220
  189.2 4.0 %copy-start.22 = (f32[128,512]{1,0:T(8,128)S(1)}, f32[128,512]{1,0:T(8,128)}, u32[]{:S(2)}) copy-start(f32[128,512]{1,0:T(8,128)} %all-reduce.3.cloned.1.call-done) | copy-start | bytes 786436
  189.2 4.0 %copy-start.38 = (f32[512]{0:T(512)S(1)}, f32[512]{0:T(512)}, u32[]{:S(2)}) copy-start(f32[512]{0:T(512)} %broadcast_bitcast_fusion.1) | copy-start | bytes 6148
  190.7 3.5 %copy-start.36 = (bf16[128,512]{1,0:T(8,128)(2,1)S(1)}, bf16[128,512]{1,0:T(8,128)(2,1)}, u32[]{:S(2)}) copy-start(bf16[128,512]{1,0:T(8,128)(2,1)} %all-reduce.4) | copy-start | bytes 393220
  195.3 12.5 %all-to-all-start = ((bf16[320,16,8]{0,2,1:T(8,128)(2,1)}), bf16[320,16,8]{0,2,1:T(8,128)(2,1)S(1)}, u32[]{:S(2)}, u32[]{:S(2)}) async-start(bf16[320,16,8]{0,2,1:T(8,128)(2,1)} %bitcast.38), calls=%async_computation | async-start | bytes 196608 | tf_op jit(solution)/shard_map/all_to_all | solution.py:122
  (10 other events, 18.2 us)
Sparse Core Ops, SparseCore 0:
  99.2 88.1 all-reduce.2
where the time goes:
time: 217 us; the launch traced here: 215 us
  blocking collectives  105 us (48%)
  matrix products  40.4 us (19%)
  local copies, waits for them, and re-layouts  31 us (14%)
  between operations  16 us (7%)
  other arithmetic  14.8 us (7%)
  starting transfers between devices  5.11 us (2%)
  waiting for transfers between devices  3.38 us (2%)
    psum x1, blocking collectives, on_device(): lax.psum((dk_n[:prompt_total], dv_n[:prompt_total]), 'cand')  63 us
    all_gather x1, blocking collectives, on_device(): lax.all_gather(prompt_key_rows, 'cand', axis=0, tiled=True)  23.7 us
    all_gather x1, blocking collectives, on_device(): lax.all_gather(prompt_value_rows, 'cand', axis=0, tiled=True)  18 us
    dot_general x8, matrix products, contract_rows(): lax.dot_general(left, right, (((0,), (0,)), ((), ())), preferred_element_...  13.6 us
    div x4, matrix products, attend(): probs = expo / jnp.sum(expo, axis=-1, keepdims=True)  10.5 us
    sub x4, matrix products, attend(): dprobs - delta  10.4 us
    dot_general x4, matrix products, attend(): jnp.dot(dscore, k_block, preferred_element_type=jnp.float32)  5.56 us
    reduce_sum x2, other arithmetic, norm_backward(): inner = jnp.mean(scaled * inputs, axis=-1, keepdims=True)  5.33 us
  transfers between devices with their start and end apart: 2, of which 1 were waited for; matrix products, arithmetic and copies ran while one was open for 14% of the time, Pallas kernels for 0%

commit v1 on v0

v1 whole, which is shorter than its diff:
```python
import functools
import math

import jax
import jax.numpy as jnp
from jax import lax
from jax.experimental import pallas as pl
from jax.experimental.pallas import tpu as pltpu
from jax.sharding import PartitionSpec as P

EPS = 1e-06
F32 = jnp.float32
BF16 = jnp.bfloat16


def dot_nt(a, b):
    return lax.dot_general(a, b, (((1,), (1,)), ((), ())), preferred_element_type=F32)


def dot_nn(a, b):
    return lax.dot_general(a, b, (((1,), (0,)), ((), ())), preferred_element_type=F32)


def kernel(
    n,
    len_ref,
    seen_ref,
    gq_ref,
    gk_ref,
    pk_hbm,
    pv_hbm,
    q_hbm,
    k_hbm,
    v_hbm,
    g_hbm,
    w_hbm,
    qo_hbm,
    ko_ref,
    vo_ref,
    ho_ref,
    pkv,
    qv,
    kv,
    vv,
    gv,
    wv,
    mask,
    dsv,
    xcv,
    kgt,
    acc,
    qo,
    rs_src,
    rs_dst,
    ag,
    hs_src,
    hs_dst,
    own_sem,
    in_sem,
    out_sem,
    pg_send,
    pg_recv,
    rs_send,
    rs_recv,
    ag_send,
    ag_recv,
    hs_send,
    hs_recv,
):
    me = lax.axis_index("cand")
    slots, q_width = qv.shape
    kv_heads = rs_src.shape[0]
    per = pkv.shape[2]
    dim = gq_ref.shape[0]
    prompt = n * per
    total = prompt + slots
    group = q_width // (kv_heads * dim)
    wide = 2 if group % 2 == 0 else 1
    pairs = group // wide
    lanes = wide * slots
    scale = dim ** (-0.5)

    own = [
        pltpu.make_async_copy(pk_hbm, pkv.at[me, 0], own_sem.at[0]),
        pltpu.make_async_copy(pv_hbm, pkv.at[me, 1], own_sem.at[1]),
    ]
    loads = [
        pltpu.make_async_copy(src, dst, in_sem.at[i])
        for i, (src, dst) in enumerate(
            ((k_hbm, kv), (v_hbm, vv), (q_hbm, qv), (g_hbm, gv), (w_hbm, wv))
        )
    ]
    for copy in own + loads:
        copy.start()

    barrier = pltpu.get_barrier_semaphore()

    def greet(step, _):
        peer = lax.rem(me + step, n)
        pl.semaphore_signal(
            barrier, inc=1, device_id={"cand": peer}, device_id_type=pl.DeviceIdType.MESH
        )
        return 0

    lax.fori_loop(1, n, greet, 0)
    pl.semaphore_wait(barrier, n - 1)

    def send_all(copy_of):
        def body(step, _):
            copy_of(lax.rem(me + step, n)).start()
            return 0

        lax.fori_loop(1, n, body, 0)

    def remote(src, dst, send, recv):
        def copy_of(peer):
            return pltpu.make_async_remote_copy(
                src_ref=src(peer),
                dst_ref=dst,
                send_sem=send,
                recv_sem=recv,
                device_id={"cand": peer},
                device_id_type=pl.DeviceIdType.MESH,
            )

        return copy_of

    def drain(buffer, sem):
        part = buffer.at[pl.ds(0, n - 1)]
        pltpu.make_async_copy(part, part, sem).wait()

    for copy in own:
        copy.wait()
    send_all(remote(lambda peer: pkv.at[me], pkv.at[me], pg_send, pg_recv))

    gq = gq_ref[...].reshape(1, dim)
    gk = gk_ref[...].reshape(1, dim)
    both = gq * gk
    row = lax.broadcasted_iota(jnp.int32, (slots, dim), 0)
    live = (row < len_ref[0]).astype(F32).astype(BF16)
    key = lax.broadcasted_iota(jnp.int32, (prompt, slots), 0)
    seen = (key < seen_ref[0]).astype(F32)
    slot_j = lax.broadcasted_iota(jnp.int32, (slots, slots), 0)
    slot_i = lax.broadcasted_iota(jnp.int32, (slots, slots), 1)
    causal = (slot_j <= slot_i).astype(F32)
    for b in range(wide):
        mask[:prompt, b * slots : (b + 1) * slots] = seen
        mask[prompt:, b * slots : (b + 1) * slots] = causal
    eye_r = lax.broadcasted_iota(jnp.int32, (dim, dim), 0)
    eye_c = lax.broadcasted_iota(jnp.int32, (dim, dim), 1)
    eye = (eye_r == eye_c).astype(F32).astype(BF16)

    def head_lanes(head):
        return pl.ds(pl.multiple_of(head * dim, dim), dim)

    def key_factor(x):
        return lax.rsqrt(jnp.mean(x * x, axis=-1, keepdims=True) + EPS)

    for copy in loads:
        copy.wait()
    drain(pkv, pg_recv)

    def forward(h, _):
        raw = jnp.concatenate(
            [
                pkv[:, 0, :, head_lanes(h)].astype(F32).reshape(prompt, dim),
                kv[:, head_lanes(h)].astype(F32),
            ],
            axis=0,
        )
        kg32 = raw * key_factor(raw) * both
        kgt[h] = kg32.T.astype(BF16)
        left = jnp.concatenate([kg32.astype(BF16), eye], axis=0)
        val = jnp.concatenate(
            [
                pkv[:, 1, :, head_lanes(h)].astype(F32).reshape(prompt, dim).astype(BF16),
                vv[:, head_lanes(h)],
            ],
            axis=0,
        )
        dk = dv = None
        for b in range(pairs):
            heads = [h * group + b * wide + a for a in range(wide)]
            x2 = jnp.concatenate([qv[:, head_lanes(a)] for a in heads], axis=0)
            g2 = jnp.concatenate([gv[:, head_lanes(a)] * live for a in heads], axis=0)
            both_t = dot_nt(left, x2)
            x_t = both_t[total:]
            r = lax.rsqrt(jnp.mean(x_t * x_t, axis=0, keepdims=True) + EPS)
            z = both_t[:total] * (r * (scale * math.log2(math.e)))
            e = jnp.exp2(z) * mask[...]
            dp = dot_nt(val, g2)
            inv = 1.0 / jnp.sum(e, axis=0, keepdims=True)
            p = e * inv
            delta = jnp.sum(p * dp, axis=0, keepdims=True)
            ds = p * (dp - delta)
            inner = jnp.sum(ds * z, axis=0, keepdims=True)
            xcv[h, b] = x_t * (r * r * inner * (math.log(2.0) / dim))
            ds = (ds * (r * scale)).astype(BF16)
            dsv[h, b] = ds
            dv_b = dot_nn(p.astype(BF16), g2)
            dk_b = dot_nn(ds, x2)
            dv = dv_b if dv is None else dv + dv_b
            dk = dk_b if dk is None else dk + dk_b
        rs_src[h, :, :, :dim] = dk[:prompt].reshape(n, per, dim).astype(BF16)
        rs_src[h, :, :, dim:] = dv[:prompt].reshape(n, per, dim).astype(BF16)
        send_all(
            remote(
                lambda peer: rs_src.at[h, peer],
                rs_dst.at[h, me],
                rs_send.at[h],
                rs_recv.at[h],
            )
        )
        rs_dst[h, me] = rs_src[h, me]
        acc[h, :, :dim] = dk[prompt:]
        acc[h, :, dim:] = dv[prompt:]
        return 0

    lax.fori_loop(0, kv_heads, forward, 0)

    def query_side(h, _):
        for b in range(pairs):
            dx = dot_nn(kgt[h], dsv[h, b]) - xcv[h, b]
            for a in range(wide):
                head = h * group + b * wide + a
                qo[:, head_lanes(head)] = dx[:, a * slots : (a + 1) * slots].T.astype(BF16)
        width = pl.ds(pl.multiple_of(h * group * dim, dim), group * dim)
        pltpu.make_async_copy(qo.at[:, width], qo_hbm.at[:, width], out_sem.at[h]).start()
        return 0

    lax.fori_loop(0, kv_heads, query_side, 0)

    def norm_back(x, upstream):
        r = key_factor(x)
        w = upstream * both
        inner = jnp.mean(w * x, axis=-1, keepdims=True)
        return r * w - x * (r * r * r) * inner

    half = kv_heads * dim
    for h in range(kv_heads):
        drain(rs_dst.at[h], rs_recv.at[h])
        sums = jnp.sum(rs_dst[h].astype(F32), axis=0)
        at = slice(h * dim, (h + 1) * dim)
        x = pkv[me, 0, :, at].astype(F32)
        w = sums[:, :dim] * gk * gq
        r = key_factor(x)
        inner = jnp.mean(w * x, axis=-1, keepdims=True)
        ag[me, :, at] = (r * w - x * (r * r * r) * inner).astype(BF16)
        ag[me, :, half + h * dim : half + (h + 1) * dim] = sums[:, dim:].astype(BF16)
    send_all(remote(lambda peer: ag.at[me], ag.at[me], ag_send, ag_recv))

    for h in range(kv_heads):
        at = slice(h * dim, (h + 1) * dim)
        ko_ref[:, at] = norm_back(kv[:, at].astype(F32), acc[h, :, :dim]).astype(BF16)
        vo_ref[:, at] = acc[h, :, dim:].astype(BF16)

    drain(ag, ag_recv)
    grads = ag[...].astype(F32).reshape(prompt, 2 * half).astype(BF16)
    piece = dot_nt(grads, wv[...])
    hs_src[...] = piece.reshape(n, per, piece.shape[1]).astype(BF16)
    send_all(remote(lambda peer: hs_src.at[peer], hs_dst.at[me], hs_send, hs_recv))
    hs_dst[me] = hs_src[me]

    def finish(h, _):
        width = pl.ds(pl.multiple_of(h * group * dim, dim), group * dim)
        pltpu.make_async_copy(qo.at[:, width], qo_hbm.at[:, width], out_sem.at[h]).wait()
        drain(rs_src.at[h], rs_send.at[h])
        return 0

    lax.fori_loop(0, kv_heads, finish, 0)
    drain(pkv, pg_send)
    drain(ag, ag_send)
    drain(hs_src, hs_send)
    drain(hs_dst, hs_recv)
    ho_ref[...] = hs_dst[...]


def solution(mesh):
    n = mesh.shape["cand"]

    def on_device(pk, pv, q, k, v, g, lengths, seen, gq, gk, w):
        dim = gq.shape[0]
        slots, q_width = q.shape
        kv_heads = k.shape[1] // dim
        group = q_width // (kv_heads * dim)
        wide = 2 if group % 2 == 0 else 1
        per = pk.shape[0]
        m = w.shape[0]
        prompt = n * per
        total = prompt + slots
        smem = pl.BlockSpec(memory_space=pltpu.SMEM)
        vmem = pl.BlockSpec(memory_space=pltpu.VMEM)
        anywhere = pl.BlockSpec(memory_space=pl.ANY)
        qo, ko, vo, ho = pl.pallas_call(
            functools.partial(kernel, n),
            out_shape=(
                jax.ShapeDtypeStruct(q.shape, BF16),
                jax.ShapeDtypeStruct(k.shape, BF16),
                jax.ShapeDtypeStruct(v.shape, BF16),
                jax.ShapeDtypeStruct((n, per, m), BF16),
            ),
            in_specs=[smem, smem, vmem, vmem] + [anywhere] * 7,
            out_specs=(anywhere, vmem, vmem, vmem),
            scratch_shapes=[
                pltpu.VMEM((n, 2) + pk.shape, BF16),
                pltpu.VMEM(q.shape, BF16),
                pltpu.VMEM(k.shape, BF16),
                pltpu.VMEM(v.shape, BF16),
                pltpu.VMEM(g.shape, BF16),
                pltpu.VMEM(w.shape, BF16),
                pltpu.VMEM((total, wide * slots), F32),
                pltpu.VMEM((kv_heads, group // wide, total, wide * slots), BF16),
                pltpu.VMEM((kv_heads, group // wide, dim, wide * slots), F32),
                pltpu.VMEM((kv_heads, dim, total), BF16),
                pltpu.VMEM((kv_heads, slots, 2 * dim), F32),
                pltpu.VMEM(q.shape, BF16),
                pltpu.VMEM((kv_heads, n, per, 2 * dim), BF16),
                pltpu.VMEM((kv_heads, n, per, 2 * dim), BF16),
                pltpu.VMEM((n, per, 2 * kv_heads * dim), BF16),
                pltpu.VMEM((n, per, m), BF16),
                pltpu.VMEM((n, per, m), BF16),
                pltpu.SemaphoreType.DMA((2,)),
                pltpu.SemaphoreType.DMA((5,)),
                pltpu.SemaphoreType.DMA((kv_heads,)),
                pltpu.SemaphoreType.DMA,
                pltpu.SemaphoreType.DMA,
                pltpu.SemaphoreType.DMA((kv_heads,)),
                pltpu.SemaphoreType.DMA((kv_heads,)),
                pltpu.SemaphoreType.DMA,
                pltpu.SemaphoreType.DMA,
                pltpu.SemaphoreType.DMA,
                pltpu.SemaphoreType.DMA,
            ],
            compiler_params=pltpu.CompilerParams(
                collective_id=0,
                has_side_effects=True,
                vmem_limit_bytes=60 * 1024 * 1024,
            ),
        )(lengths, seen, gq, gk, pk, pv, q, k, v, g, w)
        hidden = jnp.transpose(ho, (1, 0, 2)).reshape(per, n * m)
        return qo, ko, vo, hidden

    rows = P(("grp", "cand"), None)
    return jax.shard_map(
        on_device,
        mesh=mesh,
        in_specs=(rows,) * 6 + (P(("grp", "cand")), P(("grp", "cand")), P(), P(), P("cand", None)),
        out_specs=(rows,) * 4,
        check_vma=False,
    )
```

time: 217 us -> 47.5 us (0.22)
  blocking collectives: 105 us -> 0 us
  matrix products: 40.4 us -> 0 us
  Pallas kernels: 0 us -> 39.8 us
  local copies, waits for them, and re-layouts: 31 us -> 5.6 us
  other arithmetic: 14.8 us -> 0 us
  between operations: 16 us -> 1.94 us
  starting transfers between devices: 5.11 us -> 0 us
  waiting for transfers between devices: 3.38 us -> 0 us
    psum x1 -> x0, blocking collectives: 63 us -> none  [on_device(): lax.psum((dk_n[:prompt_total], dv_n[:prompt_total]), 'cand')]
    all_gather x2 -> x0, blocking collectives: 41.7 us -> none  [the longest x1 23.7 us: on_device(): lax.all_gather(prompt_key_rows, 'cand', axis=0, tiled=True)]
    pallas_call x0 -> x1, Pallas kernels: none -> 39.8 us  [on_device(): pl.pallas_call(functools.partial(kernel, n), out_shape=(jax.ShapeDtypeStr...]
    dot_general x13 -> x0, matrix products: 19.5 us -> none  [the longest x8 13.6 us: contract_rows(): lax.dot_general(left, right, (((0,), (0,)), ((), ())), preferred_element_...]
    div x4 -> x0, matrix products: 10.5 us -> none  [attend(): probs = expo / jnp.sum(expo, axis=-1, keepdims=True)]
    sub x4 -> x0, matrix products: 10.4 us -> none  [attend(): dprobs - delta]
    reshape x12 -> x1, local copies, waits for them, and re-layouts: 9.04 us -> 0.77 us  [on_device(): hidden = jnp.transpose(ho, (1, 0, 2)).reshape(per, n * m)]
    mul x10 -> x0, local copies, waits for them, and re-layouts: 7.59 us -> none  [the longest x2 2.81 us: norm_backward(): factor * factor * factor]
  transfers between devices with their start and end apart: 2 -> 0, of which waited for: 1 -> 0; matrix products, arithmetic and copies ran while one was open for 14% -> 0% of each run, Pallas kernels for 0% -> 0%
where the time goes in v1:
time: 47.5 us; the launch traced here: 47.3 us
  Pallas kernels  39.8 us (84%)
  local copies, waits for them, and re-layouts  5.6 us (12%)
  between operations  1.94 us (4%)
    pallas_call x1, Pallas kernels, on_device(): pl.pallas_call(functools.partial(kernel, n), out_shape=(jax.ShapeDtypeStr...  39.8 us
    unnamed x7, local copies, waits for them, and re-layouts  3.93 us

profile of v1, /device:TPU:0, one launch (start us, length us, event | category | flops | bytes accessed | tf_op | source)
XLA Modules:
  0.0 47.3 jit_solution(3907667597272635881)
XLA Ops:
  1.9 39.8 %shard_map.138 = (bf16[128,4096]{1,0:T(8,128)(2,1)}, bf16[128,512]{1,0:T(8,128)(2,1)}, bf16[128,512]{1,0:T(8,128)(2,1)}, bf16[16,8,320]{2,1,0:T(8,128)(2,1)}) custom-call(s32[1]{0:T(128)S(6)} %copy.19.len_ref, s32[1]{0:T(128)S(6)} %copy.20.seen_ref, f32[128]{0:T(128)} %gq_ref.1, f32[128]{0:T(128)} %gk_ref.1, bf16[8,512]{1,0:T(8,128)(2,1)} %pk_hbm.1, ...), custom_call_target="tpu_custom_call" | custom-call | tf_op jit(solution)/shard_map/pallas_call | solution.py:294
  41.7 0.9 %copy.15 = bf16[8,16,320]{2,1,0:T(8,128)(2,1)S(1)} copy(bf16[8,16,320]{2,0,1:T(8,128)(2,1)} %bitcast.1) | data formatting | bytes 163840 | tf_op jit(solution)/shard_map/transpose | solution.py:340
  42.6 0.8 %reshape.11 = bf16[8,5120]{1,0:T(8,128)(2,1)} reshape(bf16[8,16,320]{2,1,0:T(8,128)(2,1)S(1)} %copy.15) | data formatting | bytes 163840 | tf_op jit(solution)/shard_map/reshape | solution.py:340
  43.4 0.0 copy-start.1
  43.4 2.3 %copy.21 = bf16[128,4096]{1,0:T(8,128)(2,1)} copy(bf16[128,4096]{1,0:T(8,128)(2,1)} %get-tuple-element.16) | data formatting | bytes 2097152
  45.7 0.0 copy-done.1
  45.7 0.0 copy-start
  45.7 0.7 %copy.22 = bf16[128,512]{1,0:T(8,128)(2,1)} copy(bf16[128,512]{1,0:T(8,128)(2,1)S(1)} %copy-done.1) | data formatting | bytes 262144
  46.4 0.3 copy-done
  46.6 0.7 %copy.23 = bf16[128,512]{1,0:T(8,128)(2,1)} copy(bf16[128,512]{1,0:T(8,128)(2,1)S(1)} %copy-done) | data formatting | bytes 262144
Async XLA Ops:
  43.4 2.3 %copy-start.1 = (bf16[128,512]{1,0:T(8,128)(2,1)S(1)}, bf16[128,512]{1,0:T(8,128)(2,1)}, u32[]{:S(2)}) copy-start(bf16[128,512]{1,0:T(8,128)(2,1)} %get-tuple-element.17) | copy-start | bytes 393220
  45.7 1.0 %copy-start = (bf16[128,512]{1,0:T(8,128)(2,1)S(1)}, bf16[128,512]{1,0:T(8,128)(2,1)}, u32[]{:S(2)}) copy-start(bf16[128,512]{1,0:T(8,128)(2,1)} %get-tuple-element.18) | copy-start | bytes 393220

commit v2 on v1

--- a/solution.py
+++ b/solution.py
@@ -25,8 +25,8 @@
     n,
     len_ref,
     seen_ref,
-    gq_ref,
-    gk_ref,
+    gq_hbm,
+    gk_hbm,
     pk_hbm,
     pv_hbm,
     q_hbm,
@@ -34,10 +34,12 @@
     v_hbm,
     g_hbm,
     w_hbm,
-    qo_hbm,
+    qo,
     ko_ref,
     vo_ref,
     ho_ref,
+    gq_ref,
+    gk_ref,
     pkv,
     qv,
     kv,
@@ -49,7 +51,6 @@
     xcv,
     kgt,
     acc,
-    qo,
     rs_src,
     rs_dst,
     ag,
@@ -57,7 +58,6 @@
     hs_dst,
     own_sem,
     in_sem,
-    out_sem,
     pg_send,
     pg_recv,
     rs_send,
@@ -70,7 +70,7 @@
     me = lax.axis_index("cand")
     slots, q_width = qv.shape
     kv_heads = rs_src.shape[0]
-    per = pkv.shape[2]
+    per = pkv.shape[3]
     dim = gq_ref.shape[0]
     prompt = n * per
     total = prompt + slots
@@ -81,16 +81,27 @@
     scale = dim ** (-0.5)
 
     own = [
-        pltpu.make_async_copy(pk_hbm, pkv.at[me, 0], own_sem.at[0]),
-        pltpu.make_async_copy(pv_hbm, pkv.at[me, 1], own_sem.at[1]),
+        pltpu.make_async_copy(
+            src.at[:, h * dim : (h + 1) * dim], pkv.at[h, me, i], own_sem.at[i, h]
+        )
+        for i, src in enumerate((pk_hbm, pv_hbm))
+        for h in range(kv_heads)
     ]
     loads = [
         pltpu.make_async_copy(src, dst, in_sem.at[i])
         for i, (src, dst) in enumerate(
-            ((k_hbm, kv), (v_hbm, vv), (q_hbm, qv), (g_hbm, gv), (w_hbm, wv))
+            (
+                (gq_hbm, gq_ref),
+                (gk_hbm, gk_ref),
+                (k_hbm, kv),
+                (v_hbm, vv),
+                (q_hbm, qv),
+                (g_hbm, gv),
+                (w_hbm, wv),
+            )
         )
     ]
-    for copy in own + loads:
+    for copy in own:
         copy.start()
 
     barrier = pltpu.get_barrier_semaphore()
@@ -103,6 +114,8 @@
         return 0
 
     lax.fori_loop(1, n, greet, 0)
+    for copy in loads[:-1]:
+        copy.start()
     pl.semaphore_wait(barrier, n - 1)
 
     def send_all(copy_of):
@@ -131,7 +144,15 @@
 
     for copy in own:
         copy.wait()
-    send_all(remote(lambda peer: pkv.at[me], pkv.at[me], pg_send, pg_recv))
+    for h in range(kv_heads):
+        send_all(
+            remote(
+                lambda peer, h=h: pkv.at[h, me], pkv.at[h, me], pg_send.at[h], pg_recv.at[h]
+            )
+        )
+    loads[-1].start()
+    for copy in loads[:2]:
+        copy.wait()
 
     gq = gq_ref[...].reshape(1, dim)
     gk = gk_ref[...].reshape(1, dim)
@@ -156,14 +177,14 @@
     def key_factor(x):
         return lax.rsqrt(jnp.mean(x * x, axis=-1, keepdims=True) + EPS)
 
-    for copy in loads:
+    for copy in loads[2:-1]:
         copy.wait()
-    drain(pkv, pg_recv)
 
     def forward(h, _):
+        drain(pkv.at[h], pg_recv.at[h])
         raw = jnp.concatenate(
             [
-                pkv[:, 0, :, head_lanes(h)].astype(F32).reshape(prompt, dim),
+                pkv[h, :, 0].astype(F32).reshape(prompt, dim),
                 kv[:, head_lanes(h)].astype(F32),
             ],
             axis=0,
@@ -173,7 +194,7 @@
         left = jnp.concatenate([kg32.astype(BF16), eye], axis=0)
         val = jnp.concatenate(
             [
-                pkv[:, 1, :, head_lanes(h)].astype(F32).reshape(prompt, dim).astype(BF16),
+                pkv[h, :, 1].astype(F32).reshape(prompt, dim).astype(BF16),
                 vv[:, head_lanes(h)],
             ],
             axis=0,
@@ -224,8 +245,6 @@
             for a in range(wide):
                 head = h * group + b * wide + a
                 qo[:, head_lanes(head)] = dx[:, a * slots : (a + 1) * slots].T.astype(BF16)
-        width = pl.ds(pl.multiple_of(h * group * dim, dim), group * dim)
-        pltpu.make_async_copy(qo.at[:, width], qo_hbm.at[:, width], out_sem.at[h]).start()
         return 0
 
     lax.fori_loop(0, kv_heads, query_side, 0)
@@ -236,43 +255,63 @@
         inner = jnp.mean(w * x, axis=-1, keepdims=True)
         return r * w - x * (r * r * r) * inner
 
-    half = kv_heads * dim
-    for h in range(kv_heads):
-        drain(rs_dst.at[h], rs_recv.at[h])
-        sums = jnp.sum(rs_dst[h].astype(F32), axis=0)
-        at = slice(h * dim, (h + 1) * dim)
-        x = pkv[me, 0, :, at].astype(F32)
-        w = sums[:, :dim] * gk * gq
-        r = key_factor(x)
-        inner = jnp.mean(w * x, axis=-1, keepdims=True)
-        ag[me, :, at] = (r * w - x * (r * r * r) * inner).astype(BF16)
-        ag[me, :, half + h * dim : half + (h + 1) * dim] = sums[:, dim:].astype(BF16)
-    send_all(remote(lambda peer: ag.at[me], ag.at[me], ag_send, ag_recv))
-
     for h in range(kv_heads):
         at = slice(h * dim, (h + 1) * dim)
         ko_ref[:, at] = norm_back(kv[:, at].astype(F32), acc[h, :, :dim]).astype(BF16)
         vo_ref[:, at] = acc[h, :, dim:].astype(BF16)
 
-    drain(ag, ag_recv)
-    grads = ag[...].astype(F32).reshape(prompt, 2 * half).astype(BF16)
-    piece = dot_nt(grads, wv[...])
+    for h in range(kv_heads):
+        drain(rs_dst.at[h], rs_recv.at[h])
+        sums = jnp.sum(rs_dst[h].astype(F32), axis=0)
+        dk = norm_back(pkv[h, me, 0].astype(F32), sums[:, :dim])
+        ag[h, me] = jnp.concatenate([dk, sums[:, dim:]], axis=1).astype(BF16)
+        send_all(
+            remote(
+                lambda peer, h=h: ag.at[h, me], ag.at[h, me], ag_send.at[h], ag_recv.at[h]
+            )
+        )
+
+    loads[-1].wait()
+    half = kv_heads * dim
+    piece = None
+    for h in range(kv_heads):
+        drain(ag.at[h], ag_recv.at[h])
+        grads = ag[h].astype(F32).reshape(prompt, 2 * dim).astype(BF16)
+        at = slice(h * dim, (h + 1) * dim)
+        w_h = jnp.concatenate(
+            [wv[:, at], wv[:, half + h * dim : half + (h + 1) * dim]], axis=1
+        )
+        part = dot_nt(grads, w_h)
+        piece = part if piece is None else piece + part
     hs_src[...] = piece.reshape(n, per, piece.shape[1]).astype(BF16)
     send_all(remote(lambda peer: hs_src.at[peer], hs_dst.at[me], hs_send, hs_recv))
     hs_dst[me] = hs_src[me]
 
     def finish(h, _):
-        width = pl.ds(pl.multiple_of(h * group * dim, dim), group * dim)
-        pltpu.make_async_copy(qo.at[:, width], qo_hbm.at[:, width], out_sem.at[h]).wait()
         drain(rs_src.at[h], rs_send.at[h])
+        drain(pkv.at[h], pg_send.at[h])
+        drain(ag.at[h], ag_send.at[h])
         return 0
 
     lax.fori_loop(0, kv_heads, finish, 0)
-    drain(pkv, pg_send)
-    drain(ag, ag_send)
     drain(hs_src, hs_send)
     drain(hs_dst, hs_recv)
     ho_ref[...] = hs_dst[...]
+
+
+def write_out(qo, ko, vo, ho, q_hbm, k_hbm, v_hbm, h_hbm, hidden, sem):
+    copies = [
+        pltpu.make_async_copy(src, dst, sem.at[i])
+        for i, (src, dst) in enumerate(((qo, q_hbm), (ko, k_hbm), (vo, v_hbm), (hidden, h_hbm)))
+    ]
+    for copy in copies[:3]:
+        copy.start()
+    hidden[...] = jnp.concatenate(
+        [ho[i].astype(F32) for i in range(ho.shape[0])], axis=1
+    ).astype(BF16)
+    copies[3].start()
+    for copy in copies:
+        copy.wait()
 
 
 def solution(mesh):
@@ -294,15 +333,17 @@
         qo, ko, vo, ho = pl.pallas_call(
             functools.partial(kernel, n),
             out_shape=(
-                jax.ShapeDtypeStruct(q.shape, BF16),
-                jax.ShapeDtypeStruct(k.shape, BF16),
-                jax.ShapeDtypeStruct(v.shape, BF16),
-                jax.ShapeDtypeStruct((n, per, m), BF16),
+                pltpu.VMEM(q.shape, BF16),
+                pltpu.VMEM(k.shape, BF16),
+                pltpu.VMEM(v.shape, BF16),
+                pltpu.VMEM((n, per, m), BF16),
             ),
-            in_specs=[smem, smem, vmem, vmem] + [anywhere] * 7,
-            out_specs=(anywhere, vmem, vmem, vmem),
+            in_specs=[smem] * 2 + [pl.BlockSpec(memory_space=pltpu.HBM)] * 9,
+            out_specs=(vmem,) * 4,
             scratch_shapes=[
-                pltpu.VMEM((n, 2) + pk.shape, BF16),
+                pltpu.VMEM(gq.shape, F32),
+                pltpu.VMEM(gk.shape, F32),
+                pltpu.VMEM((kv_heads, n, 2, per, dim), BF16),
                 pltpu.VMEM(q.shape, BF16),
                 pltpu.VMEM(k.shape, BF16),
                 pltpu.VMEM(v.shape, BF16),
@@ -313,32 +354,45 @@
                 pltpu.VMEM((kv_heads, group // wide, dim, wide * slots), F32),
                 pltpu.VMEM((kv_heads, dim, total), BF16),
                 pltpu.VMEM((kv_heads, slots, 2 * dim), F32),
-                pltpu.VMEM(q.shape, BF16),
                 pltpu.VMEM((kv_heads, n, per, 2 * dim), BF16),
                 pltpu.VMEM((kv_heads, n, per, 2 * dim), BF16),
-                pltpu.VMEM((n, per, 2 * kv_heads * dim), BF16),
+                pltpu.VMEM((kv_heads, n, per, 2 * dim), BF16),
                 pltpu.VMEM((n, per, m), BF16),
                 pltpu.VMEM((n, per, m), BF16),
-                pltpu.SemaphoreType.DMA((2,)),
-                pltpu.SemaphoreType.DMA((5,)),
-                pltpu.SemaphoreType.DMA((kv_heads,)),
-                pltpu.SemaphoreType.DMA,
-                pltpu.SemaphoreType.DMA,
-                pltpu.SemaphoreType.DMA((kv_heads,)),
-                pltpu.SemaphoreType.DMA((kv_heads,)),
-                pltpu.SemaphoreType.DMA,
-                pltpu.SemaphoreType.DMA,
-                pltpu.SemaphoreType.DMA,
-                pltpu.SemaphoreType.DMA,
-            ],
+                pltpu.SemaphoreType.DMA((2, kv_heads)),
+                pltpu.SemaphoreType.DMA((7,)),
+            ]
+            + [pltpu.SemaphoreType.DMA((kv_heads,))] * 6
+            + [pltpu.SemaphoreType.DMA] * 2,
             compiler_params=pltpu.CompilerParams(
                 collective_id=0,
                 has_side_effects=True,
-                vmem_limit_bytes=60 * 1024 * 1024,
+                vmem_limit_bytes=48 * 1024 * 1024,
             ),
-        )(lengths, seen, gq, gk, pk, pv, q, k, v, g, w)
-        hidden = jnp.transpose(ho, (1, 0, 2)).reshape(per, n * m)
-        return qo, ko, vo, hidden
+        )(
+            lengths,
+            seen,
+            *[
+                pltpu.with_memory_space_constraint(x, pltpu.HBM)
+                for x in (gq, gk, pk, pv, q, k, v, g, w)
+            ],
+        )
+        return pl.pallas_call(
+            write_out,
+            out_shape=(
+                jax.ShapeDtypeStruct(q.shape, BF16),
+                jax.ShapeDtypeStruct(k.shape, BF16),
+                jax.ShapeDtypeStruct(v.shape, BF16),
+                jax.ShapeDtypeStruct((per, n * m), BF16),
+            ),
+            in_specs=[vmem] * 4,
+            out_specs=(anywhere,) * 4,
+            scratch_shapes=[
+                pltpu.VMEM((per, n * m), BF16),
+                pltpu.SemaphoreType.DMA((4,)),
+            ],
+            compiler_params=pltpu.CompilerParams(vmem_limit_bytes=8 * 1024 * 1024),
+        )(*[pltpu.with_memory_space_constraint(x, pltpu.VMEM) for x in (qo, ko, vo, ho)])
 
     rows = P(("grp", "cand"), None)
     return jax.shard_map(

time: 47.5 us -> 35.8 us (0.75)
  Pallas kernels: 39.8 us -> 33.7 us
  local copies, waits for them, and re-layouts: 5.6 us -> 0 us
    pallas_call x1 -> x2, Pallas kernels: 39.8 us -> 33.7 us  [the longest x1 32.6 us: on_device(): pl.pallas_call(functools.partial(kernel, n), out_shape=(pltpu.VMEM(q.shap...]
    unnamed x7 -> x0, local copies, waits for them, and re-layouts: 3.93 us -> none
    transpose x1 -> x0, local copies, waits for them, and re-layouts: 0.91 us -> none  [on_device(): hidden = jnp.transpose(ho, (1, 0, 2)).reshape(per, n * m)]
    reshape x1 -> x0, local copies, waits for them, and re-layouts: 0.77 us -> none  [on_device(): hidden = jnp.transpose(ho, (1, 0, 2)).reshape(per, n * m)]
where the time goes in v2:
time: 35.8 us; the launch traced here: 35.6 us
  Pallas kernels  33.7 us (94%)
  between operations  1.93 us (5%)
    pallas_call x1, Pallas kernels, on_device(): pl.pallas_call(functools.partial(kernel, n), out_shape=(pltpu.VMEM(q.shap...  32.6 us
    pallas_call x1, Pallas kernels, on_device(): pl.pallas_call(write_out, out_shape=(jax.ShapeDtypeStruct(q.shape, BF16),...  1.1 us

profile of v2, /device:TPU:0, one launch (start us, length us, event | category | flops | bytes accessed | tf_op | source)
XLA Modules:
  0.0 35.6 jit_solution(6433486769732070234)
XLA Ops:
  1.9 32.6 %shard_map.138 = (bf16[128,4096]{1,0:T(8,128)(2,1)S(1)}, bf16[128,512]{1,0:T(8,128)(2,1)S(1)}, bf16[128,512]{1,0:T(8,128)(2,1)S(1)}, bf16[16,8,320]{2,1,0:T(8,128)(2,1)S(1)}) custom-call(s32[1]{0:T(128)S(6)} %copy.15.len_ref, s32[1]{0:T(128)S(6)} %copy.16.seen_ref, f32[128]{0:T(128)} %gq_hbm.1, f32[128]{0:T(128)} %gk_hbm.1, bf16[8,512]{1,0:T(8,128)(2,1)} %pk_hbm.1, ...), custom_call_target="tpu_custom_call" | custom-call | tf_op jit(solution)/shard_map/pallas_call | solution.py:333
  34.5 1.1 %shard_map.139 = (bf16[128,4096]{1,0:T(8,128)(2,1)}, bf16[128,512]{1,0:T(8,128)(2,1)}, bf16[128,512]{1,0:T(8,128)(2,1)}, bf16[8,5120]{1,0:T(8,128)(2,1)}) custom-call(bf16[128,4096]{1,0:T(8,128)(2,1)S(1)} %get-tuple-element.8.qo, bf16[128,512]{1,0:T(8,128)(2,1)S(1)} %get-tuple-element.9.ko, bf16[128,512]{1,0:T(8,128)(2,1)S(1)} %get-tuple-element.10.vo, ...), custom_call_target="tpu_custom_call" | custom-call | tf_op jit(solution)/shard_map/pallas_call | solution.py:380

commit v3 on v2

--- a/solution.py
+++ b/solution.py
@@ -47,6 +47,9 @@
     gv,
     wv,
     mask,
+    ev,
+    dpv,
+    pv,
     dsv,
     xcv,
     kgt,
@@ -78,6 +81,7 @@
     wide = 2 if group % 2 == 0 else 1
     pairs = group // wide
     lanes = wide * slots
+    chunk = math.gcd(total, 64)
     scale = dim ** (-0.5)
 
     own = [
@@ -199,29 +203,38 @@
             ],
             axis=0,
         )
-        dk = dv = None
+        heads = [qv[:, head_lanes(h * group + a)] for a in range(group)]
+        x_all = jnp.concatenate(heads, axis=0)
+        heads = [gv[:, head_lanes(h * group + a)] * live for a in range(group)]
+        g_all = jnp.concatenate(heads, axis=0)
         for b in range(pairs):
-            heads = [h * group + b * wide + a for a in range(wide)]
-            x2 = jnp.concatenate([qv[:, head_lanes(a)] for a in heads], axis=0)
-            g2 = jnp.concatenate([gv[:, head_lanes(a)] * live for a in heads], axis=0)
-            both_t = dot_nt(left, x2)
+            at = slice(b * lanes, (b + 1) * lanes)
+            both_t = dot_nt(left, x_all[at])
+            ev[b] = both_t[:total]
             x_t = both_t[total:]
             r = lax.rsqrt(jnp.mean(x_t * x_t, axis=0, keepdims=True) + EPS)
-            z = both_t[:total] * (r * (scale * math.log2(math.e)))
-            e = jnp.exp2(z) * mask[...]
-            dp = dot_nt(val, g2)
-            inv = 1.0 / jnp.sum(e, axis=0, keepdims=True)
-            p = e * inv
-            delta = jnp.sum(p * dp, axis=0, keepdims=True)
-            ds = p * (dp - delta)
-            inner = jnp.sum(ds * z, axis=0, keepdims=True)
-            xcv[h, b] = x_t * (r * r * inner * (math.log(2.0) / dim))
-            ds = (ds * (r * scale)).astype(BF16)
-            dsv[h, b] = ds
-            dv_b = dot_nn(p.astype(BF16), g2)
-            dk_b = dot_nn(ds, x2)
-            dv = dv_b if dv is None else dv + dv_b
-            dk = dk_b if dk is None else dk + dk_b
+            xcv[h, :, at] = x_t * r
+            dpv[b] = dot_nt(val, g_all[at])
+            up = r * (scale * math.log2(math.e))
+            tops = inner = jnp.zeros((8, lanes), F32)
+            for c in range(0, total, chunk):
+                rows = slice(c, c + chunk)
+                e = jnp.exp2(ev[b, rows] * up) * mask[rows]
+                ev[b, rows] = e
+                tops = tops + jnp.sum(e.reshape(chunk // 8, 8, lanes), axis=0)
+                inner = inner + jnp.sum(
+                    (e * dpv[b, rows]).reshape(chunk // 8, 8, lanes), axis=0
+                )
+            inv = 1.0 / jnp.sum(tops, axis=0, keepdims=True)
+            delta = jnp.sum(inner, axis=0, keepdims=True) * inv
+            down = inv * (r * scale)
+            for c in range(0, total, chunk):
+                rows = slice(c, c + chunk)
+                e = ev[b, rows]
+                pv[rows, at] = (e * inv).astype(BF16)
+                dsv[h, rows, at] = (e * (dpv[b, rows] - delta) * down).astype(BF16)
+        dv = dot_nn(pv[...], g_all)
+        dk = dot_nn(dsv[h], x_all)
         rs_src[h, :, :, :dim] = dk[:prompt].reshape(n, per, dim).astype(BF16)
         rs_src[h, :, :, dim:] = dv[:prompt].reshape(n, per, dim).astype(BF16)
         send_all(
@@ -241,7 +254,10 @@
 
     def query_side(h, _):
         for b in range(pairs):
-            dx = dot_nn(kgt[h], dsv[h, b]) - xcv[h, b]
+            at = slice(b * lanes, (b + 1) * lanes)
+            dq = dot_nn(kgt[h], dsv[h, :, at])
+            x_t = xcv[h, :, at]
+            dx = dq - x_t * jnp.mean(dq * x_t, axis=0, keepdims=True)
             for a in range(wide):
                 head = h * group + b * wide + a
                 qo[:, head_lanes(head)] = dx[:, a * slots : (a + 1) * slots].T.astype(BF16)
@@ -350,8 +366,11 @@
                 pltpu.VMEM(g.shape, BF16),
                 pltpu.VMEM(w.shape, BF16),
                 pltpu.VMEM((total, wide * slots), F32),
-                pltpu.VMEM((kv_heads, group // wide, total, wide * slots), BF16),
-                pltpu.VMEM((kv_heads, group // wide, dim, wide * slots), F32),
+                pltpu.VMEM((group // wide, total, wide * slots), F32),
+                pltpu.VMEM((group // wide, total, wide * slots), F32),
+                pltpu.VMEM((total, group * slots), BF16),
+                pltpu.VMEM((kv_heads, total, group * slots), BF16),
+                pltpu.VMEM((kv_heads, dim, group * slots), F32),
                 pltpu.VMEM((kv_heads, dim, total), BF16),
                 pltpu.VMEM((kv_heads, slots, 2 * dim), F32),
                 pltpu.VMEM((kv_heads, n, per, 2 * dim), BF16),

time: 35.8 us -> 34.5 us (0.964)
  Pallas kernels: 33.7 us -> 32.4 us
    pallas_call x1, Pallas kernels: 32.6 us -> 31.3 us  [on_device(): pl.pallas_call(functools.partial(kernel, n), out_shape=(pltpu.VMEM(q.shap...]
where the time goes in v3:
time: 34.5 us; the launch traced here: 34.3 us
  Pallas kernels  32.4 us (94%)
  between operations  1.93 us (6%)
    pallas_call x1, Pallas kernels, on_device(): pl.pallas_call(functools.partial(kernel, n), out_shape=(pltpu.VMEM(q.shap...  31.3 us
    pallas_call x1, Pallas kernels, on_device(): pl.pallas_call(write_out, out_shape=(jax.ShapeDtypeStruct(q.shape, BF16),...  1.1 us

profile of v3, /device:TPU:0, one launch (start us, length us, event | category | flops | bytes accessed | tf_op | source)
XLA Modules:
  0.0 34.3 jit_solution(5678341597218225586)
XLA Ops:
  1.9 31.3 %shard_map.138 = (bf16[128,4096]{1,0:T(8,128)(2,1)S(1)}, bf16[128,512]{1,0:T(8,128)(2,1)S(1)}, bf16[128,512]{1,0:T(8,128)(2,1)S(1)}, bf16[16,8,320]{2,1,0:T(8,128)(2,1)S(1)}) custom-call(s32[1]{0:T(128)S(6)} %copy.15.len_ref, s32[1]{0:T(128)S(6)} %copy.16.seen_ref, f32[128]{0:T(128)} %gq_hbm.1, f32[128]{0:T(128)} %gk_hbm.1, bf16[8,512]{1,0:T(8,128)(2,1)} %pk_hbm.1, ...), custom_call_target="tpu_custom_call" | custom-call | tf_op jit(solution)/shard_map/pallas_call | solution.py:349
  33.2 1.1 %shard_map.139 = (bf16[128,4096]{1,0:T(8,128)(2,1)}, bf16[128,512]{1,0:T(8,128)(2,1)}, bf16[128,512]{1,0:T(8,128)(2,1)}, bf16[8,5120]{1,0:T(8,128)(2,1)}) custom-call(bf16[128,4096]{1,0:T(8,128)(2,1)S(1)} %get-tuple-element.8.qo, bf16[128,512]{1,0:T(8,128)(2,1)S(1)} %get-tuple-element.9.ko, bf16[128,512]{1,0:T(8,128)(2,1)S(1)} %get-tuple-element.10.vo, ...), custom_call_target="tpu_custom_call" | custom-call | tf_op jit(solution)/shard_map/pallas_call | solution.py:399

commit v4 on v3

--- a/solution.py
+++ b/solution.py
@@ -49,7 +49,11 @@
     mask,
     ev,
     dpv,
+    er,
+    dpr,
     pv,
+    rv,
+    sums_v,
     dsv,
     xcv,
     kgt,
@@ -81,7 +85,7 @@
     wide = 2 if group % 2 == 0 else 1
     pairs = group // wide
     lanes = wide * slots
-    chunk = math.gcd(total, 64)
+    chunk = math.gcd(math.gcd(prompt, slots), 64)
     scale = dim ** (-0.5)
 
     own = [
@@ -117,7 +121,7 @@
         )
         return 0
 
-    lax.fori_loop(1, n, greet, 0)
+    lax.fori_loop(1, n, greet, 0, unroll=n <= 16)
     for copy in loads[:-1]:
         copy.start()
     pl.semaphore_wait(barrier, n - 1)
@@ -127,7 +131,7 @@
             copy_of(lax.rem(me + step, n)).start()
             return 0
 
-        lax.fori_loop(1, n, body, 0)
+        lax.fori_loop(1, n, body, 0, unroll=n <= 16)
 
     def remote(src, dst, send, recv):
         def copy_of(peer):
@@ -184,55 +188,76 @@
     for copy in loads[2:-1]:
         copy.wait()
 
-    def forward(h, _):
-        drain(pkv.at[h], pg_recv.at[h])
-        raw = jnp.concatenate(
-            [
-                pkv[h, :, 0].astype(F32).reshape(prompt, dim),
-                kv[:, head_lanes(h)].astype(F32),
-            ],
-            axis=0,
-        )
-        kg32 = raw * key_factor(raw) * both
-        kgt[h] = kg32.T.astype(BF16)
-        left = jnp.concatenate([kg32.astype(BF16), eye], axis=0)
-        val = jnp.concatenate(
-            [
-                pkv[h, :, 1].astype(F32).reshape(prompt, dim).astype(BF16),
-                vv[:, head_lanes(h)],
-            ],
-            axis=0,
-        )
+    def load_heads(h):
         heads = [qv[:, head_lanes(h * group + a)] for a in range(group)]
         x_all = jnp.concatenate(heads, axis=0)
         heads = [gv[:, head_lanes(h * group + a)] * live for a in range(group)]
-        g_all = jnp.concatenate(heads, axis=0)
+        return x_all, jnp.concatenate(heads, axis=0)
+
+    def lift(h, at, e_ref, dp_ref, first, tops, inner):
+        up = rv[h, :, at] * (scale * math.log2(math.e))
+        for c in range(0, e_ref.shape[0], chunk):
+            rows = slice(c, c + chunk)
+            e = jnp.exp2(e_ref[rows] * up) * mask[first + c : first + c + chunk]
+            e_ref[rows] = e
+            tops = tops + jnp.sum(e.reshape(chunk // 8, 8, lanes), axis=0)
+            inner = inner + jnp.sum(
+                (e * dp_ref[rows]).reshape(chunk // 8, 8, lanes), axis=0
+            )
+        return tops, inner
+
+    def respond(h, _):
+        raw = kv[:, head_lanes(h)].astype(F32)
+        kg32 = raw * key_factor(raw) * both
+        kgt[h, :, prompt:] = kg32.T.astype(BF16)
+        left = jnp.concatenate([kg32.astype(BF16), eye], axis=0)
+        val = vv[:, head_lanes(h)]
+        x_all, g_all = load_heads(h)
         for b in range(pairs):
             at = slice(b * lanes, (b + 1) * lanes)
             both_t = dot_nt(left, x_all[at])
-            ev[b] = both_t[:total]
-            x_t = both_t[total:]
+            er[h, b] = both_t[:slots]
+            x_t = both_t[slots:]
             r = lax.rsqrt(jnp.mean(x_t * x_t, axis=0, keepdims=True) + EPS)
+            rv[h, :, at] = r
             xcv[h, :, at] = x_t * r
+            dpr[h, b] = dot_nt(val, g_all[at])
+            zero = jnp.zeros((8, lanes), F32)
+            tops, inner = lift(h, at, er.at[h, b], dpr.at[h, b], prompt, zero, zero)
+            sums_v[h, 0, :, at] = tops
+            sums_v[h, 1, :, at] = inner
+        return 0
+
+    lax.fori_loop(0, kv_heads, respond, 0)
+
+    def forward(h, _):
+        drain(pkv.at[h], pg_recv.at[h])
+        raw = pkv[h, :, 0].astype(F32).reshape(prompt, dim)
+        kg32 = raw * key_factor(raw) * both
+        kgt[h, :, :prompt] = kg32.T.astype(BF16)
+        left = kg32.astype(BF16)
+        val = pkv[h, :, 1].astype(F32).reshape(prompt, dim).astype(BF16)
+        x_all, g_all = load_heads(h)
+        for b in range(pairs):
+            at = slice(b * lanes, (b + 1) * lanes)
+            ev[b] = dot_nt(left, x_all[at])
             dpv[b] = dot_nt(val, g_all[at])
-            up = r * (scale * math.log2(math.e))
-            tops = inner = jnp.zeros((8, lanes), F32)
-            for c in range(0, total, chunk):
-                rows = slice(c, c + chunk)
-                e = jnp.exp2(ev[b, rows] * up) * mask[rows]
-                ev[b, rows] = e
-                tops = tops + jnp.sum(e.reshape(chunk // 8, 8, lanes), axis=0)
-                inner = inner + jnp.sum(
-                    (e * dpv[b, rows]).reshape(chunk // 8, 8, lanes), axis=0
-                )
+            tops, inner = lift(
+                h, at, ev.at[b], dpv.at[b], 0, sums_v[h, 0, :, at], sums_v[h, 1, :, at]
+            )
             inv = 1.0 / jnp.sum(tops, axis=0, keepdims=True)
             delta = jnp.sum(inner, axis=0, keepdims=True) * inv
-            down = inv * (r * scale)
-            for c in range(0, total, chunk):
-                rows = slice(c, c + chunk)
-                e = ev[b, rows]
-                pv[rows, at] = (e * inv).astype(BF16)
-                dsv[h, rows, at] = (e * (dpv[b, rows] - delta) * down).astype(BF16)
+            down = inv * (rv[h, :, at] * scale)
+            for first, e_ref, dp_ref in (
+                (0, ev.at[b], dpv.at[b]),
+                (prompt, er.at[h, b], dpr.at[h, b]),
+            ):
+                for c in range(0, e_ref.shape[0], chunk):
+                    rows = slice(c, c + chunk)
+                    to = slice(first + c, first + c + chunk)
+                    e = e_ref[rows]
+                    pv[to, at] = (e * inv).astype(BF16)
+                    dsv[h, to, at] = (e * (dp_ref[rows] - delta) * down).astype(BF16)
         dv = dot_nn(pv[...], g_all)
         dk = dot_nn(dsv[h], x_all)
         rs_src[h, :, :, :dim] = dk[:prompt].reshape(n, per, dim).astype(BF16)
@@ -366,9 +391,13 @@
                 pltpu.VMEM(g.shape, BF16),
                 pltpu.VMEM(w.shape, BF16),
                 pltpu.VMEM((total, wide * slots), F32),
-                pltpu.VMEM((group // wide, total, wide * slots), F32),
-                pltpu.VMEM((group // wide, total, wide * slots), F32),
+                pltpu.VMEM((group // wide, prompt, wide * slots), F32),
+                pltpu.VMEM((group // wide, prompt, wide * slots), F32),
+                pltpu.VMEM((kv_heads, group // wide, slots, wide * slots), F32),
+                pltpu.VMEM((kv_heads, group // wide, slots, wide * slots), F32),
                 pltpu.VMEM((total, group * slots), BF16),
+                pltpu.VMEM((kv_heads, 1, group * slots), F32),
+                pltpu.VMEM((kv_heads, 2, 8, group * slots), F32),
                 pltpu.VMEM((kv_heads, total, group * slots), BF16),
                 pltpu.VMEM((kv_heads, dim, group * slots), F32),
                 pltpu.VMEM((kv_heads, dim, total), BF16),

time: 34.5 us -> 33.2 us (0.962)
  Pallas kernels: 32.4 us -> 31.1 us
    pallas_call x1, Pallas kernels: 31.3 us -> 30 us  [on_device(): pl.pallas_call(functools.partial(kernel, n), out_shape=(pltpu.VMEM(q.shap...]
where the time goes in v4:
time: 33.2 us; the launch traced here: 33 us
  Pallas kernels  31.1 us (94%)
  between operations  1.93 us (6%)
    pallas_call x1, Pallas kernels, on_device(): pl.pallas_call(functools.partial(kernel, n), out_shape=(pltpu.VMEM(q.shap...  30 us
    pallas_call x1, Pallas kernels, on_device(): pl.pallas_call(write_out, out_shape=(jax.ShapeDtypeStruct(q.shape, BF16),...  1.1 us

profile of v4, /device:TPU:0, one launch (start us, length us, event | category | flops | bytes accessed | tf_op | source)
XLA Modules:
  0.0 33.0 jit_solution(17349279804687611196)
XLA Ops:
  1.9 30.0 %shard_map.138 = (bf16[128,4096]{1,0:T(8,128)(2,1)S(1)}, bf16[128,512]{1,0:T(8,128)(2,1)S(1)}, bf16[128,512]{1,0:T(8,128)(2,1)S(1)}, bf16[16,8,320]{2,1,0:T(8,128)(2,1)S(1)}) custom-call(s32[1]{0:T(128)S(6)} %copy.15.len_ref, s32[1]{0:T(128)S(6)} %copy.16.seen_ref, f32[128]{0:T(128)} %gq_hbm.1, f32[128]{0:T(128)} %gk_hbm.1, bf16[8,512]{1,0:T(8,128)(2,1)} %pk_hbm.1, ...), custom_call_target="tpu_custom_call" | custom-call | tf_op jit(solution)/shard_map/pallas_call | solution.py:374
  31.9 1.1 %shard_map.139 = (bf16[128,4096]{1,0:T(8,128)(2,1)}, bf16[128,512]{1,0:T(8,128)(2,1)}, bf16[128,512]{1,0:T(8,128)(2,1)}, bf16[8,5120]{1,0:T(8,128)(2,1)}) custom-call(bf16[128,4096]{1,0:T(8,128)(2,1)S(1)} %get-tuple-element.8.qo, bf16[128,512]{1,0:T(8,128)(2,1)S(1)} %get-tuple-element.9.ko, bf16[128,512]{1,0:T(8,128)(2,1)S(1)} %get-tuple-element.10.vo, ...), custom_call_target="tpu_custom_call" | custom-call | tf_op jit(solution)/shard_map/pallas_call | solution.py:428

commit v5 on v4

--- a/solution.py
+++ b/solution.py
@@ -57,7 +57,8 @@
     dsv,
     xcv,
     kgt,
-    acc,
+    pr,
+    stats,
     rs_src,
     rs_dst,
     ag,
@@ -248,20 +249,17 @@
             inv = 1.0 / jnp.sum(tops, axis=0, keepdims=True)
             delta = jnp.sum(inner, axis=0, keepdims=True) * inv
             down = inv * (rv[h, :, at] * scale)
-            for first, e_ref, dp_ref in (
-                (0, ev.at[b], dpv.at[b]),
-                (prompt, er.at[h, b], dpr.at[h, b]),
-            ):
-                for c in range(0, e_ref.shape[0], chunk):
-                    rows = slice(c, c + chunk)
-                    to = slice(first + c, first + c + chunk)
-                    e = e_ref[rows]
-                    pv[to, at] = (e * inv).astype(BF16)
-                    dsv[h, to, at] = (e * (dp_ref[rows] - delta) * down).astype(BF16)
+            for i, value in enumerate((inv, delta, down)):
+                stats[h, i, :, at] = value
+            for c in range(0, prompt, chunk):
+                rows = slice(c, c + chunk)
+                e = ev[b, rows]
+                pv[rows, at] = (e * inv).astype(BF16)
+                dsv[h, rows, at] = (e * (dpv[b, rows] - delta) * down).astype(BF16)
         dv = dot_nn(pv[...], g_all)
-        dk = dot_nn(dsv[h], x_all)
-        rs_src[h, :, :, :dim] = dk[:prompt].reshape(n, per, dim).astype(BF16)
-        rs_src[h, :, :, dim:] = dv[:prompt].reshape(n, per, dim).astype(BF16)
+        dk = dot_nn(dsv[h, :prompt], x_all)
+        rs_src[h, :, :, :dim] = dk.reshape(n, per, dim).astype(BF16)
+        rs_src[h, :, :, dim:] = dv.reshape(n, per, dim).astype(BF16)
         send_all(
             remote(
                 lambda peer: rs_src.at[h, peer],
@@ -271,35 +269,41 @@
             )
         )
         rs_dst[h, me] = rs_src[h, me]
-        acc[h, :, :dim] = dk[prompt:]
-        acc[h, :, dim:] = dv[prompt:]
         return 0
 
     lax.fori_loop(0, kv_heads, forward, 0)
 
+    def norm_back(x, upstream):
+        r = key_factor(x)
+        w = upstream * both
+        inner = jnp.mean(w * x, axis=-1, keepdims=True)
+        return r * w - x * (r * r * r) * inner
+
     def query_side(h, _):
+        x_all, g_all = load_heads(h)
         for b in range(pairs):
             at = slice(b * lanes, (b + 1) * lanes)
+            inv, delta, down = [stats[h, i, :, at] for i in range(3)]
+            for c in range(0, slots, chunk):
+                rows = slice(c, c + chunk)
+                e = er[h, b, rows]
+                pr[rows, at] = (e * inv).astype(BF16)
+                dsv[h, prompt + c : prompt + c + chunk, at] = (
+                    e * (dpr[h, b, rows] - delta) * down
+                ).astype(BF16)
             dq = dot_nn(kgt[h], dsv[h, :, at])
             x_t = xcv[h, :, at]
             dx = dq - x_t * jnp.mean(dq * x_t, axis=0, keepdims=True)
             for a in range(wide):
                 head = h * group + b * wide + a
                 qo[:, head_lanes(head)] = dx[:, a * slots : (a + 1) * slots].T.astype(BF16)
+        dk = dot_nn(dsv[h, prompt:], x_all)
+        at = head_lanes(h)
+        ko_ref[:, at] = norm_back(kv[:, at].astype(F32), dk).astype(BF16)
+        vo_ref[:, at] = dot_nn(pr[...], g_all).astype(BF16)
         return 0
 
     lax.fori_loop(0, kv_heads, query_side, 0)
-
-    def norm_back(x, upstream):
-        r = key_factor(x)
-        w = upstream * both
-        inner = jnp.mean(w * x, axis=-1, keepdims=True)
-        return r * w - x * (r * r * r) * inner
-
-    for h in range(kv_heads):
-        at = slice(h * dim, (h + 1) * dim)
-        ko_ref[:, at] = norm_back(kv[:, at].astype(F32), acc[h, :, :dim]).astype(BF16)
-        vo_ref[:, at] = acc[h, :, dim:].astype(BF16)
 
     for h in range(kv_heads):
         drain(rs_dst.at[h], rs_recv.at[h])
@@ -395,13 +399,14 @@
                 pltpu.VMEM((group // wide, prompt, wide * slots), F32),
                 pltpu.VMEM((kv_heads, group // wide, slots, wide * slots), F32),
                 pltpu.VMEM((kv_heads, group // wide, slots, wide * slots), F32),
-                pltpu.VMEM((total, group * slots), BF16),
+                pltpu.VMEM((prompt, group * slots), BF16),
                 pltpu.VMEM((kv_heads, 1, group * slots), F32),
                 pltpu.VMEM((kv_heads, 2, 8, group * slots), F32),
                 pltpu.VMEM((kv_heads, total, group * slots), BF16),
                 pltpu.VMEM((kv_heads, dim, group * slots), F32),
                 pltpu.VMEM((kv_heads, dim, total), BF16),
-                pltpu.VMEM((kv_heads, slots, 2 * dim), F32),
+                pltpu.VMEM((slots, group * slots), BF16),
+                pltpu.VMEM((kv_heads, 3, 1, group * slots), F32),
                 pltpu.VMEM((kv_heads, n, per, 2 * dim), BF16),
                 pltpu.VMEM((kv_heads, n, per, 2 * dim), BF16),
                 pltpu.VMEM((kv_heads, n, per, 2 * dim), BF16),

time: 33.2 us -> 33.2 us (level)
  no operation moved by 1% of the time
where the time goes in v5:
time: 33.2 us; the launch traced here: 33 us
  Pallas kernels  31.1 us (94%)
  between operations  1.93 us (6%)
    pallas_call x1, Pallas kernels, on_device(): pl.pallas_call(functools.partial(kernel, n), out_shape=(pltpu.VMEM(q.shap...  30 us
    pallas_call x1, Pallas kernels, on_device(): pl.pallas_call(write_out, out_shape=(jax.ShapeDtypeStruct(q.shape, BF16),...  1.1 us

profile of v5, /device:TPU:0, one launch (start us, length us, event | category | flops | bytes accessed | tf_op | source)
XLA Modules:
  0.0 33.0 jit_solution(4899338065731608275)
XLA Ops:
  1.9 30.0 %shard_map.138 = (bf16[128,4096]{1,0:T(8,128)(2,1)S(1)}, bf16[128,512]{1,0:T(8,128)(2,1)S(1)}, bf16[128,512]{1,0:T(8,128)(2,1)S(1)}, bf16[16,8,320]{2,1,0:T(8,128)(2,1)S(1)}) custom-call(s32[1]{0:T(128)S(6)} %copy.15.len_ref, s32[1]{0:T(128)S(6)} %copy.16.seen_ref, f32[128]{0:T(128)} %gq_hbm.1, f32[128]{0:T(128)} %gk_hbm.1, bf16[8,512]{1,0:T(8,128)(2,1)} %pk_hbm.1, ...), custom_call_target="tpu_custom_call" | custom-call | tf_op jit(solution)/shard_map/pallas_call | solution.py:378
  31.9 1.1 %shard_map.139 = (bf16[128,4096]{1,0:T(8,128)(2,1)}, bf16[128,512]{1,0:T(8,128)(2,1)}, bf16[128,512]{1,0:T(8,128)(2,1)}, bf16[8,5120]{1,0:T(8,128)(2,1)}) custom-call(bf16[128,4096]{1,0:T(8,128)(2,1)S(1)} %get-tuple-element.8.qo, bf16[128,512]{1,0:T(8,128)(2,1)S(1)} %get-tuple-element.9.ko, bf16[128,512]{1,0:T(8,128)(2,1)S(1)} %get-tuple-element.10.vo, ...), custom_call_target="tpu_custom_call" | custom-call | tf_op jit(solution)/shard_map/pallas_call | solution.py:433
